TPU v7x, 32 devices: a whole 2x2x4 slice. The times are simulated.
32 devices in a mesh: freq: 2 (over x), facet: 16 (over z, y, core).
Axes of the slice: x: 2, y: 2, z: 4, core: 2. Of those that a mesh axis runs over, the one named last changes fastest.
Arguments:
- model_image: float32 [128, 2048], P('facet'), may hold values from -6 to 6
- visibilities: float32 [2, 8192], P(None, ('freq', 'facet')), may hold values from -6 to 6
- kernel_u: float32 [16, 8192], P(None, ('freq', 'facet')), may hold values from -1.5 to 1.5
- kernel_v: float32 [16, 8192], P(None, ('freq', 'facet')), may hold values from -1.5 to 1.5
- owners: int32 [8192, 1], P(('freq', 'facet')), may hold values from 0 to 15; in each aligned block of 256 rows (0 to 255, 256 to 511, ...) at most 64 rows name the same one
- offsets: int32 [2, 8192], P(None, ('freq', 'facet')), may hold values from 0 to 48
- corners: int32 [2, 16, 2], P('freq'), may hold values from -8192 to 8128
Outputs:
- model_out: float32 [128, 2048], P('facet')
- residual_rows: float32 [2, 8192], P(None, ('freq', 'facet'))
Inputs may be any that keep to these rules, and one draw needn't show every extreme that they name: `owners`: within each device's 256 rows, at most 64 rows name one owner, a bound that some block reaches of them.
All inputs are finite; a program needn't handle non-finite values.
Results may differ from a plain program's by a relative error of at most 0.0045.
Values sent between devices are 32-bit elements; how exact they have to be, the bound alone decides.
No kernel may reach another device: no remote copies, remote signals or barrier semaphores. Data moves between devices by JAX's collectives and lax.ppermute only.
A program may use at most 64 MiB of HBM per device.

v0:
```python
import math
import jax
import jax.numpy as jnp
from jax import lax
from jax.sharding import PartitionSpec as P

GRID = 16384
FACET = 2048
FROWS = 8
SUB = 64
SUPPORT = 16
CYCLES = 2
exact_products = lax.Precision.HIGHEST
GAIN_STEP = 0.5


def phase_pair(freq_index, position):
    angle_value = jnp.mod(freq_index * position, GRID).astype(jnp.float32) * (2.0 * math.pi / GRID)
    return (jnp.cos(angle_value), jnp.sin(angle_value))


def column_table():
    columns = jnp.arange(FACET, dtype=jnp.int32)
    frequency = jnp.arange(SUB, dtype=jnp.int32)
    cos_t, sin_t = phase_pair(frequency[None, :], columns[:, None])
    return jnp.concatenate([cos_t, sin_t], axis=1)


def make_back(col_table):
    cos_t = col_table[:, :SUB].T
    sin_t = col_table[:, SUB:].T
    upper = jnp.concatenate([cos_t, sin_t], axis=1)
    lower = jnp.concatenate([-sin_t, cos_t], axis=1)
    return jnp.concatenate([upper, lower], axis=0)


def forward_part(images, facet_ids, u_start, v_start, col_table):
    amount = images.shape[0]
    columns = jnp.arange(FACET, dtype=jnp.int32)
    cos_u, sin_u = phase_pair(u_start, columns)
    real_mod = (images * cos_u).reshape(amount * FROWS, FACET).astype(jnp.bfloat16)
    imag_mod = (-images * sin_u).reshape(amount * FROWS, FACET).astype(jnp.bfloat16)
    table_half = col_table.astype(jnp.bfloat16)
    real_prod = jnp.dot(real_mod, table_half, preferred_element_type=jnp.float32).reshape(
        amount, FROWS, 2 * SUB
    )
    imag_prod = jnp.dot(imag_mod, table_half, preferred_element_type=jnp.float32).reshape(
        amount, FROWS, 2 * SUB
    )
    col_re = real_prod[..., :SUB] + imag_prod[..., SUB:]
    col_im = imag_prod[..., :SUB] - real_prod[..., SUB:]
    frequency = jnp.arange(SUB, dtype=jnp.int32)
    x_start = facet_ids % (GRID // FACET) * FACET - GRID // 2
    cos_x, sin_x = phase_pair(u_start + frequency[None, :], x_start[:, None])
    shift_re = col_re * cos_x[:, None, :] + col_im * sin_x[:, None, :]
    shift_im = col_im * cos_x[:, None, :] - col_re * sin_x[:, None, :]
    y_pos = (facet_ids // (GRID // FACET) * FACET - GRID // 2)[:, None] + jnp.arange(
        FROWS, dtype=jnp.int32
    )[None, :]
    cosine_vertical, sine_vertical = phase_pair(v_start + frequency[:, None, None], y_pos[None])
    grid_re = jnp.einsum(
        "bfr,fra->ba", cosine_vertical, shift_re, precision=exact_products
    ) + jnp.einsum("bfr,fra->ba", sine_vertical, shift_im, precision=exact_products)
    grid_im = jnp.einsum(
        "bfr,fra->ba", cosine_vertical, shift_im, precision=exact_products
    ) - jnp.einsum("bfr,fra->ba", sine_vertical, shift_re, precision=exact_products)
    return jnp.stack([grid_re, grid_im], axis=1)


def forward_sum(images, facet_ids, u_start, v_start, col_table):
    amount = images.shape[0]
    blocking = math.gcd(amount, 8)

    def forward_accumulate(running, pieces):
        return (running + forward_part(pieces[0], pieces[1], u_start, v_start, col_table), None)

    sectioned = images.reshape(amount // blocking, blocking, FROWS, FACET)
    sectioned_ids = facet_ids.reshape(amount // blocking, blocking)
    running, unused = lax.scan(
        forward_accumulate, jnp.zeros((SUB, 2, SUB), jnp.float32), (sectioned, sectioned_ids)
    )
    return running


def adjoint_part(blocks, u_starts, v_starts, facet_here, back_table):
    amount = blocks.shape[0]
    frequency = jnp.arange(SUB, dtype=jnp.int32)
    y_pos = facet_here // (GRID // FACET) * FACET - GRID // 2 + jnp.arange(FROWS, dtype=jnp.int32)
    cosine_vertical, sine_vertical = phase_pair(
        v_starts[:, None, None] + frequency[None, :, None], y_pos[None, None, :]
    )
    kernel_real = blocks[:, :, 0, :]
    kernel_imaginary = blocks[:, :, 1, :]
    row_real = jnp.einsum(
        "gil,gik->glk", cosine_vertical, kernel_real, precision=exact_products
    ) - jnp.einsum("gil,gik->glk", sine_vertical, kernel_imaginary, precision=exact_products)
    row_imaginary = jnp.einsum(
        "gil,gik->glk", cosine_vertical, kernel_imaginary, precision=exact_products
    ) + jnp.einsum("gil,gik->glk", sine_vertical, kernel_real, precision=exact_products)
    x_start = facet_here % (GRID // FACET) * FACET - GRID // 2
    cos_x, sin_x = phase_pair(u_starts[:, None] + frequency[None, :], x_start)
    shift_re = row_real * cos_x[:, None, :] - row_imaginary * sin_x[:, None, :]
    shift_im = row_imaginary * cos_x[:, None, :] + row_real * sin_x[:, None, :]
    joined = (
        jnp.concatenate([shift_re, shift_im], axis=2)
        .reshape(amount * FROWS, 2 * SUB)
        .astype(jnp.bfloat16)
    )
    both = jnp.dot(
        joined, back_table.astype(jnp.bfloat16), preferred_element_type=jnp.float32
    ).reshape(amount, FROWS, 2 * FACET)
    columns = jnp.arange(FACET, dtype=jnp.int32)
    cos_u, sin_u = phase_pair(u_starts[:, None], columns[None, :])
    return jnp.sum(
        both[..., :FACET] * cos_u[:, None, :] - both[..., FACET:] * sin_u[:, None, :], axis=0
    )


def adjoint_sum(blocks, corner_list, facet_here, back_table):
    amount = blocks.shape[0]
    blocking = math.gcd(amount, 8)

    def adjoint_accumulate(running, pieces):
        return (
            running
            + adjoint_part(pieces[0], pieces[1][:, 0], pieces[1][:, 1], facet_here, back_table),
            None,
        )

    sectioned = blocks.reshape(amount // blocking, blocking, SUB, 2, SUB)
    starts = corner_list.reshape(amount // blocking, blocking, 2)
    running, unused = lax.scan(
        adjoint_accumulate, jnp.zeros((FROWS, FACET), jnp.float32), (sectioned, starts)
    )
    return running


def slot_positions(owner_ids, capacity, owner_count):
    owner_hits = (owner_ids[:, None] == jnp.arange(owner_count, dtype=jnp.int32)[None, :]).astype(
        jnp.int32
    )
    before = jnp.cumsum(owner_hits, axis=0) - owner_hits
    return owner_ids * capacity + jnp.sum(before * owner_hits, axis=1)


def place_kernel(kernel, offset_row):
    row_ids = jnp.arange(SUB, dtype=jnp.int32)[:, None]
    placed = jnp.zeros((SUB, kernel.shape[1]), jnp.float32)
    for kernel_tap in range(SUPPORT):
        placed = placed + jnp.where(
            row_ids == offset_row[None, :] + kernel_tap, kernel[kernel_tap][None, :], 0.0
        )
    return placed


def predict_rows(grid_block, kern_u, kern_v):
    partial_rows = jnp.einsum("bpa,ar->bpr", grid_block, kern_u, precision=exact_products)
    return jnp.sum(kern_v[:, None, :] * partial_rows, axis=0)


def grid_rows(residual, kern_u, kern_v):
    return jnp.einsum(
        "br,par->bpa", kern_v, residual[:, None, :] * kern_u[None], precision=exact_products
    )


def on_device(model_image, visibilities, kernel_u, kernel_v, owners, offsets, corners):
    facet_count = lax.axis_size("facet")
    facet_here = lax.axis_index("facet")
    device_rows = owners.shape[0]
    capacity = 4 * device_rows // facet_count
    scale = 1.0 / math.sqrt(facet_count * FROWS * FACET)
    slot_index = slot_positions(owners[:, 0], capacity, facet_count)
    payload = jnp.concatenate(
        [visibilities, kernel_u, kernel_v, offsets.astype(jnp.float32)], axis=0
    )
    feature_rows = payload.shape[0]
    send_buffer = (
        jnp.zeros((feature_rows, facet_count * capacity), jnp.float32)
        .at[:, slot_index]
        .set(payload)
    )
    send_buffer = send_buffer.reshape(feature_rows, facet_count, capacity)
    arrived = lax.all_to_all(send_buffer, "facet", split_axis=1, concat_axis=1, tiled=True).reshape(
        feature_rows, facet_count * capacity
    )
    observed = arrived[0:2]
    kern_u = place_kernel(arrived[2 : 2 + SUPPORT], arrived[2 + 2 * SUPPORT].astype(jnp.int32))
    kern_v = place_kernel(
        arrived[2 + SUPPORT : 2 + 2 * SUPPORT], arrived[3 + 2 * SUPPORT].astype(jnp.int32)
    )
    corner_list = corners[0]
    own_corner = corner_list[facet_here]
    col_table = column_table()
    back_table = make_back(col_table)
    current = model_image
    residual = observed
    for major_cycle in range(CYCLES):
        gathered = lax.all_gather(current, "facet", axis=0, tiled=True)
        amount = gathered.shape[0] // FROWS
        facet_ids = jnp.arange(amount, dtype=jnp.int32)
        summed = forward_sum(
            gathered.reshape(amount, FROWS, FACET),
            facet_ids,
            own_corner[0],
            own_corner[1],
            col_table,
        )
        grid_block = scale * summed
        residual = observed - predict_rows(grid_block, kern_u, kern_v)
        gridded = grid_rows(residual, kern_u, kern_v)
        add_gathered = lax.all_gather(gridded, "facet", axis=0, tiled=True)
        add_amount = add_gathered.shape[0] // SUB
        dirty_image = scale * adjoint_sum(
            add_gathered.reshape(add_amount, SUB, 2, SUB), corner_list, facet_here, back_table
        )
        current = current + GAIN_STEP * lax.psum(dirty_image, "freq")
    returned = lax.all_to_all(
        residual.reshape(2, facet_count, capacity), "facet", split_axis=1, concat_axis=1, tiled=True
    )
    returned = returned.reshape(2, facet_count * capacity)
    return (current, returned[:, slot_index])


def solution(mesh):
    return jax.shard_map(
        on_device,
        mesh=mesh,
        in_specs=(
            P("facet", None),
            P(None, ("freq", "facet")),
            P(None, ("freq", "facet")),
            P(None, ("freq", "facet")),
            P(("freq", "facet"), None),
            P(None, ("freq", "facet")),
            P("freq", None, None),
        ),
        out_specs=(P("facet", None), P(None, ("freq", "facet"))),
        check_vma=False,
    )
```

profile of v0, /device:TPU:0, one launch (start us, length us, event | category | flops | bytes accessed | tf_op | source)
XLA Modules:
  0.0 240.4 jit_solution(4313704084468116243)
XLA Ops:
  11.6 1.3 scatter_custom_fusion
  14.1 7.4 %all-to-all-start = ((f32[16,1,2304]{2,1,0:T(1,128)}), f32[16,1,2304]{2,1,0:T(1,128)S(1)}, u32[]{:S(2)}, u32[]{:S(2)}) async-start(f32[16,1,2304]{2,1,0:T(1,128)} %reshape.2303), calls=%async_computation | async-start | bytes 294912 | tf_op jit(solution)/shard_map/all_to_all | solution.py:184
  22.3 2.2 negate_convert_fusion
  24.4 2.0 fusion.234
  27.1 4.4 %sine_convert_fusion = (bf16[2048,64]{1,0:T(8,128)(2,1)S(1)}, bf16[2048,64]{1,0:T(8,128)(2,1)S(1)}) fusion(), kind=kLoop, calls=%fused_computation.325 | loop fusion | flops 2097152 | bytes 524288 | tf_op jit(solution)/shard_map/convert.11
  38.1 25.6 %all-gather.3.cloned.1.call-done = f32[128,2048]{1,0:T(8,128)} async-done(((f32[8,2048]{1,0:T(8,128)}), f32[128,2048]{1,0:T(8,128)}) %all-gather.3.cloned.1.call-update) | async-done | bytes 1048592 | tf_op jit(solution)/shard_map/all_gather | solution.py:199
  63.7 11.2 %while.58 = (s32[]{:T(128)}, f32[64,2,64]{2,0,1:T(8,128)S(1)}, s32[]{:T(128)}, s32[2,8]{1,0:T(2,128)S(1)}, f32[2,8,8,2048]{3,2,1,0:T(8,128)}, /*index=5*/s32[]{:...) while((s32[]{:T(128)}, f32[64,2,64]{2,0,1:T(8,128)S(1)}, s32[]{:T(128)}, ...), condition=%wide.region_5.6_spmd.clone, body=%wide.region_4.5_spmd.clone.sunk | while | flops 80678272 | bytes 6762359 | solution.py:79
  64.5 1.3 fusion.336
  70.1 1.3 fusion.336
  71.7 1.2 iota_add_fusion.18
  76.4 22.5 %all_gather.13 = f32[1024,2,64]{2,0,1:T(8,128)S(1)} all-gather(f32[64,2,64]{2,0,1:T(8,128)S(1)} %fusion.225), channel_id=1, replica_groups=mesh['freq'=2,'facet'=16] {'facet'}, dimensions={0}, use_global_device_ids=true | all-gather | bytes 557056 | tf_op jit(solution)/shard_map/all_gather | solution.py:212
  98.9 6.5 %while.59 = (s32[]{:T(128)}, f32[8,2048]{1,0:T(8,128)S(1)}, s32[2,8,2]{1,2,0:T(2,128)S(1)}, s32[]{:T(128)}, f32[2,8,64,2,64]{4,2,1,0,3:T(8,128)S(1)}, /*index=5*...) while((s32[]{:T(128)}, f32[8,2048]{1,0:T(8,128)S(1)}, s32[2,8,2]{1,2,0:T(2,128)S(1)}, ...), condition=%wide.region_9.10_spmd.clone, body=%wide.region_7.9_spmd.clone.sunk | while | flops 80773128 | bytes 5456375 | solution.py:132
  106.1 18.3 %all-reduce.3.cloned.1.call-done = f32[8,2048]{1,0:T(8,128)} async-done(((f32[8,2048]{1,0:T(8,128)}), f32[8,2048]{1,0:T(8,128)}) %all-reduce.3.cloned.1.call-update) | async-done | bytes 65552 | tf_op jit(solution)/shard_map/psum | solution.py:217
  124.4 1.5 multiply_add_fusion.5
  125.9 39.1 %all-gather.5.cloned.1.call-done = f32[128,2048]{1,0:T(8,128)} async-done(((f32[8,2048]{1,0:T(8,128)}), f32[128,2048]{1,0:T(8,128)}) %all-gather.5.cloned.1.call-update) | async-done | bytes 1048592 | tf_op jit(solution)/shard_map/all_gather | solution.py:199
  165.0 11.2 %while.60 = (s32[]{:T(128)}, f32[64,2,64]{2,0,1:T(8,128)S(1)}, s32[]{:T(128)}, s32[2,8]{1,0:T(2,128)S(1)}, f32[2,8,8,2048]{3,2,1,0:T(8,128)}, /*index=5*/s32[]{:...) while((s32[]{:T(128)}, f32[64,2,64]{2,0,1:T(8,128)S(1)}, s32[]{:T(128)}, ...), condition=%wide.region_12.13_spmd.clone, body=%wide.region_11.12_spmd.clone.sunk | while | flops 80678272 | bytes 6762359 | solution.py:79
  165.8 1.3 fusion.366
  171.4 1.3 fusion.366
  173.0 1.2 iota_add_fusion.22
  177.7 3.7 %all-to-all-start.1 = ((f32[16,1,128]{2,1,0:T(1,128)}), f32[16,1,128]{2,1,0:T(1,128)S(1)}, u32[]{:S(2)}, u32[]{:S(2)}) async-start(f32[16,1,128]{2,1,0:T(1,128)} %reshape.2305), calls=%async_computation.1 | async-start | bytes 16384 | tf_op jit(solution)/shard_map/all_to_all | solution.py:218
  182.3 24.6 %all_gather.15 = f32[1024,2,64]{2,0,1:T(8,128)S(1)} all-gather(f32[64,2,64]{2,0,1:T(8,128)S(1)} %fusion.221), channel_id=1, replica_groups=mesh['freq'=2,'facet'=16] {'facet'}, dimensions={0}, use_global_device_ids=true | all-gather | bytes 557056 | tf_op jit(solution)/shard_map/all_gather | solution.py:212
  206.9 6.5 %while.61 = (s32[]{:T(128)}, f32[8,2048]{1,0:T(8,128)S(1)}, s32[2,8,2]{1,2,0:T(2,128)S(1)}, s32[]{:T(128)}, f32[2,8,64,2,64]{4,2,1,0,3:T(8,128)S(1)}, /*index=5*...) while((s32[]{:T(128)}, f32[8,2048]{1,0:T(8,128)S(1)}, ...), condition=%wide.region_16.17_spmd.clone, body=%wide.region_14.16_spmd.clone.sunk | while | flops 80773128 | bytes 5456375 | solution.py:132
  216.5 15.9 %all-reduce.5.cloned.1.call-done = f32[8,2048]{1,0:T(8,128)} async-done(((f32[8,2048]{1,0:T(8,128)}), f32[8,2048]{1,0:T(8,128)}) %all-reduce.5.cloned.1.call-update) | async-done | bytes 65552 | tf_op jit(solution)/shard_map/psum | solution.py:217
  232.4 1.5 multiply_add_fusion.4
  (218 shorter events, 48.3 us)
Async XLA Ops:
  12.9 13.5 %copy-start.4 = (s32[1,16,2]{1,2,0:T(2,128)S(1)}, s32[1,16,2]{1,2,0:T(2,128)}, u32[]{:S(2)}) copy-start(s32[1,16,2]{1,2,0:T(2,128)} %param.21) | copy-start | bytes 388
  14.1 17.9 %all-to-all-start = ((f32[16,1,2304]{2,1,0:T(1,128)}), f32[16,1,2304]{2,1,0:T(1,128)S(1)}, u32[]{:S(2)}, u32[]{:S(2)}) async-start(f32[16,1,2304]{2,1,0:T(1,128)} %reshape.2303), calls=%async_computation | async-start | bytes 294912 | tf_op jit(solution)/shard_map/all_to_all | solution.py:184
  21.5 42.2 %all-gather.3.cloned.1.call-start = ((), (), s32[]{:S(2)}) async-start(), calls=%async_computation.2 | async-start | bytes 1114112 | tf_op jit(solution)/shard_map/all_gather | solution.py:199
  22.2 102.2 %all-reduce.3.cloned.1.call-start = ((), (), s32[]{:S(2)}) async-start(), calls=%async_computation.3 | async-start | bytes 131072 | tf_op jit(solution)/shard_map/psum | solution.py:217
  63.7 2.1 copy-start
  69.3 2.1 copy-start
  98.9 25.5 %copy-start.3 = (f32[8,2048]{1,0:T(8,128)S(1)}, f32[8,2048]{1,0:T(8,128)}, u32[]{:S(2)}) copy-start(f32[8,2048]{1,0:T(8,128)} %param.15) | copy-start | bytes 196612
  106.1 59.0 %all-gather.5.cloned.1.call-start = ((), (), s32[]{:S(2)}) async-start(), calls=%async_computation.4 | async-start | bytes 1114112 | tf_op jit(solution)/shard_map/all_gather | solution.py:199
  165.0 2.1 copy-start.1
  170.6 2.1 copy-start.1
  177.7 36.4 %all-to-all-start.1 = ((f32[16,1,128]{2,1,0:T(1,128)}), f32[16,1,128]{2,1,0:T(1,128)S(1)}, u32[]{:S(2)}, u32[]{:S(2)}) async-start(f32[16,1,128]{2,1,0:T(1,128)} %reshape.2305), calls=%async_computation.1 | async-start | bytes 16384 | tf_op jit(solution)/shard_map/all_to_all | solution.py:218
  181.3 51.0 %all-reduce.5.cloned.1.call-start = ((), (), s32[]{:S(2)}) async-start(), calls=%async_computation.5 | async-start | bytes 131072 | tf_op jit(solution)/shard_map/psum | solution.py:217
  206.9 25.5 %copy-start.2 = (f32[8,2048]{1,0:T(8,128)S(1)}, f32[8,2048]{1,0:T(8,128)}, u32[]{:S(2)}) copy-start(f32[8,2048]{1,0:T(8,128)} %multiply_add_fusion.5) | copy-start | bytes 196612
Sparse Core Ops, SparseCore 0:
  24.4 39.2 all-gather.2
  106.2 18.1 all-reduce.2
  127.1 37.8 all-gather.4
  214.2 18.1 all-reduce.4
where the time goes:
time: 241 us; the launch traced here: 240 us
  waiting for transfers between devices  99.6 us (41%)
  blocking collectives  47.1 us (20%)
  other arithmetic  32.1 us (13%)
  matrix products  25.6 us (11%)
  between operations  14.1 us (6%)
  starting transfers between devices  11.3 us (5%)
  local copies, waits for them, and re-layouts  10 us (4%)
    all_gather x2, waiting for transfers between devices, on_device(): gathered = lax.all_gather(current, 'facet', axis=0, tiled=True)  64.7 us
    all_gather x2, blocking collectives, on_device(): add_gathered = lax.all_gather(gridded, 'facet', axis=0, tiled=True)  47.1 us
    psum x2, waiting for transfers between devices, on_device(): current = current + GAIN_STEP * lax.psum(dirty_image, 'freq')  34.2 us
    another operation x5, other arithmetic  9.08 us
    all_to_all x1, starting transfers between devices, on_device(): lax.all_to_all(send_buffer, 'facet', split_axis=1, concat_axis=1, tiled=T...  7.41 us
    dot_general x4, matrix products, forward_part(): jnp.dot(imag_mod, table_half, preferred_element_type=jnp.float32)  5.08 us
  transfers between devices with their start and end apart: 6, of which 4 were waited for; matrix products, arithmetic and copies ran while one was open for 11% of the time, Pallas kernels for 0%

commit v1 on v0

--- a/solution.py
+++ b/solution.py
@@ -214,7 +214,7 @@
         dirty_image = scale * adjoint_sum(
             add_gathered.reshape(add_amount, SUB, 2, SUB), corner_list, facet_here, back_table
         )
-        current = current + GAIN_STEP * lax.psum(dirty_image, "freq")
+        current = current + GAIN_STEP * jnp.sum(lax.all_gather(dirty_image, "freq"), axis=0)
     returned = lax.all_to_all(
         residual.reshape(2, facet_count, capacity), "facet", split_axis=1, concat_axis=1, tiled=True
     )

time: 241 us -> 210 us (0.87)
  waiting for transfers between devices: 99.6 us -> 61.5 us
  blocking collectives: 47.1 us -> 57.2 us
  other arithmetic: 32.1 us -> 29.1 us
    psum x2 -> x0, waiting for transfers between devices: 34.2 us -> none  [on_device(): current = current + GAIN_STEP * lax.psum(dirty_image, 'freq')]
    all_gather x0 -> x2, blocking collectives: none -> 10 us  [on_device(): lax.all_gather(dirty_image, 'freq')]
    all_gather x2, waiting for transfers between devices: 64.7 us -> 60.8 us  [on_device(): gathered = lax.all_gather(current, 'facet', axis=0, tiled=True)]
  transfers between devices with their start and end apart: 6 -> 4, of which waited for: 4 -> 2; matrix products, arithmetic and copies ran while one was open for 11% -> 11% of each run, Pallas kernels for 0% -> 0%
where the time goes in v1:
time: 210 us
  waiting for transfers between devices  61.5 us (29%)
  blocking collectives  57.2 us (27%)
  other arithmetic  29.1 us (14%)
  matrix products  25.5 us (12%)
  between operations  14.4 us (7%)
  starting transfers between devices  11.2 us (5%)
  local copies, waits for them, and re-layouts  10 us (5%)
    all_gather x2, waiting for transfers between devices, on_device(): gathered = lax.all_gather(current, 'facet', axis=0, tiled=True)  60.8 us
    all_gather x2, blocking collectives, on_device(): add_gathered = lax.all_gather(gridded, 'facet', axis=0, tiled=True)  47.1 us
    all_gather x2, blocking collectives, on_device(): lax.all_gather(dirty_image, 'freq')  10 us
    another operation x5, other arithmetic  9.08 us
    all_to_all x1, starting transfers between devices, on_device(): lax.all_to_all(send_buffer, 'facet', split_axis=1, concat_axis=1, tiled=T...  7.41 us
    dot_general x4, matrix products, forward_part(): jnp.dot(imag_mod, table_half, preferred_element_type=jnp.float32)  5.06 us
    add x4, other arithmetic, forward_part(): cos_x, sin_x = phase_pair(u_start + frequency[None, :], x_start[:, None])  4.8 us
  transfers between devices with their start and end apart: 4, of which 2 were waited for; matrix products, arithmetic and copies ran while one was open for 11% of the time, Pallas kernels for 0%

profile of v1, /device:TPU:0, one launch (start us, length us, event | category | flops | bytes accessed | tf_op | source)
XLA Modules:
  0.0 209.6 jit_solution(17887064475293622601)
XLA Ops:
  11.6 1.3 scatter_custom_fusion
  14.1 7.4 %all-to-all-start = ((f32[16,1,2304]{2,1,0:T(1,128)}), f32[16,1,2304]{2,1,0:T(1,128)S(1)}, u32[]{:S(2)}, u32[]{:S(2)}) async-start(f32[16,1,2304]{2,1,0:T(1,128)} %reshape.2305), calls=%async_computation | async-start | bytes 294912 | tf_op jit(solution)/shard_map/all_to_all | solution.py:184
  22.3 2.2 %negate_convert_fusion = (bf16[64,2048]{1,0:T(8,128)(2,1)S(1)}, bf16[64,2048]{1,0:T(8,128)(2,1)S(1)}) fusion(), kind=kLoop, calls=%fused_computation.339 | loop fusion | flops 2228224 | bytes 524288 | tf_op jit(solution)/shard_map/convert.6
  24.4 2.0 fusion.234
  27.1 4.4 %sine_convert_fusion = (bf16[2048,64]{1,0:T(8,128)(2,1)S(1)}, bf16[2048,64]{1,0:T(8,128)(2,1)S(1)}) fusion(), kind=kLoop, calls=%fused_computation.325 | loop fusion | flops 2097152 | bytes 524288 | tf_op jit(solution)/shard_map/convert.11
  38.1 25.6 %all-gather.5.cloned.1.call-done = f32[128,2048]{1,0:T(8,128)} async-done(((f32[8,2048]{1,0:T(8,128)}), f32[128,2048]{1,0:T(8,128)}) %all-gather.5.cloned.1.call-update) | async-done | bytes 1048592 | tf_op jit(solution)/shard_map/all_gather | solution.py:199
  63.7 11.2 %while.58 = (s32[]{:T(128)}, f32[64,2,64]{2,0,1:T(8,128)S(1)}, s32[]{:T(128)}, s32[2,8]{1,0:T(2,128)S(1)}, f32[2,8,8,2048]{3,2,1,0:T(8,128)}, /*index=5*/s32[]{:...) while((s32[]{:T(128)}, f32[64,2,64]{2,0,1:T(8,128)S(1)}, s32[]{:T(128)}, ...), condition=%wide.region_5.6_spmd.clone, body=%wide.region_4.5_spmd.clone.sunk | while | flops 80678272 | bytes 6762359 | solution.py:79
  64.5 1.3 fusion.336
  66.0 1.2 iota_add_fusion.18
  70.1 1.3 fusion.336
  71.7 1.2 iota_add_fusion.18
  76.4 22.5 %all_gather.25 = f32[1024,2,64]{2,0,1:T(8,128)S(1)} all-gather(f32[64,2,64]{2,0,1:T(8,128)S(1)} %fusion.225), channel_id=1, replica_groups=mesh['freq'=2,'facet'=16] {'facet'}, dimensions={0}, use_global_device_ids=true | all-gather | bytes 557056 | tf_op jit(solution)/shard_map/all_gather | solution.py:212
  98.9 6.5 %while.59 = (s32[]{:T(128)}, f32[8,2048]{1,0:T(8,128)S(1)}, s32[2,8,2]{1,2,0:T(2,128)S(1)}, s32[]{:T(128)}, f32[2,8,64,2,64]{4,2,1,0,3:T(8,128)S(1)}, /*index=5*...) while((s32[]{:T(128)}, f32[8,2048]{1,0:T(8,128)S(1)}, s32[2,8,2]{1,2,0:T(2,128)S(1)}, ...), condition=%wide.region_9.10_spmd.clone, body=%wide.region_7.9_spmd.clone.sunk | while | flops 80773128 | bytes 5456375 | solution.py:132
  105.4 5.0 %all-gather = f32[16,2048]{1,0:T(8,128)S(1)} all-gather(f32[8,2048]{1,0:T(8,128)S(1)} %broadcast_multiply_fusion.1), channel_id=2, replica_groups=mesh['freq'=2,'facet'=16] {'freq'}, dimensions={0}, use_global_device_ids=true | all-gather | bytes 196608 | tf_op jit(solution)/shard_map/all_gather | solution.py:217
  111.1 35.2 %all-gather.7.cloned.1.call-done = f32[128,2048]{1,0:T(8,128)} async-done(((f32[8,2048]{1,0:T(8,128)}), f32[128,2048]{1,0:T(8,128)}) %all-gather.7.cloned.1.call-update) | async-done | bytes 1048592 | tf_op jit(solution)/shard_map/all_gather | solution.py:199
  146.3 11.2 %while.60 = (s32[]{:T(128)}, f32[64,2,64]{2,0,1:T(8,128)S(1)}, s32[]{:T(128)}, s32[2,8]{1,0:T(2,128)S(1)}, f32[2,8,8,2048]{3,2,1,0:T(8,128)}, /*index=5*/s32[]{:...) while((s32[]{:T(128)}, f32[64,2,64]{2,0,1:T(8,128)S(1)}, s32[]{:T(128)}, ...), condition=%wide.region_12.13_spmd.clone, body=%wide.region_11.12_spmd.clone.sunk | while | flops 80678272 | bytes 6762359 | solution.py:79
  147.1 1.3 fusion.366
  148.7 1.2 iota_add_fusion.22
  152.7 1.3 fusion.366
  154.3 1.2 iota_add_fusion.22
  159.0 3.7 %all-to-all-start.1 = ((f32[16,1,128]{2,1,0:T(1,128)}), f32[16,1,128]{2,1,0:T(1,128)S(1)}, u32[]{:S(2)}, u32[]{:S(2)}) async-start(f32[16,1,128]{2,1,0:T(1,128)} %reshape.2307), calls=%async_computation.1 | async-start | bytes 16384 | tf_op jit(solution)/shard_map/all_to_all | solution.py:218
  163.5 24.6 %all_gather.29 = f32[1024,2,64]{2,0,1:T(8,128)S(1)} all-gather(f32[64,2,64]{2,0,1:T(8,128)S(1)} %fusion.221), channel_id=1, replica_groups=mesh['freq'=2,'facet'=16] {'facet'}, dimensions={0}, use_global_device_ids=true | all-gather | bytes 557056 | tf_op jit(solution)/shard_map/all_gather | solution.py:212
  188.2 6.5 %while.61 = (s32[]{:T(128)}, f32[8,2048]{1,0:T(8,128)S(1)}, s32[2,8,2]{1,2,0:T(2,128)S(1)}, s32[]{:T(128)}, f32[2,8,64,2,64]{4,2,1,0,3:T(8,128)S(1)}, /*index=5*...) while((s32[]{:T(128)}, f32[8,2048]{1,0:T(8,128)S(1)}, ...), condition=%wide.region_16.17_spmd.clone, body=%wide.region_14.16_spmd.clone.sunk | while | flops 80773128 | bytes 5456375 | solution.py:132
  194.7 5.0 %all-gather.1 = f32[16,2048]{1,0:T(8,128)S(1)} all-gather(f32[8,2048]{1,0:T(8,128)S(1)} %broadcast_multiply_fusion), channel_id=3, replica_groups=mesh['freq'=2,'facet'=16] {'freq'}, dimensions={0}, use_global_device_ids=true | all-gather | bytes 196608 | tf_op jit(solution)/shard_map/all_gather | solution.py:217
  (216 shorter events, 45.8 us)
Async XLA Ops:
  12.9 13.5 %copy-start.4 = (s32[1,16,2]{1,2,0:T(2,128)S(1)}, s32[1,16,2]{1,2,0:T(2,128)}, u32[]{:S(2)}) copy-start(s32[1,16,2]{1,2,0:T(2,128)} %param.21) | copy-start | bytes 388
  14.1 17.9 %all-to-all-start = ((f32[16,1,2304]{2,1,0:T(1,128)}), f32[16,1,2304]{2,1,0:T(1,128)S(1)}, u32[]{:S(2)}, u32[]{:S(2)}) async-start(f32[16,1,2304]{2,1,0:T(1,128)} %reshape.2305), calls=%async_computation | async-start | bytes 294912 | tf_op jit(solution)/shard_map/all_to_all | solution.py:184
  21.5 42.2 %all-gather.5.cloned.1.call-start = ((), (), s32[]{:S(2)}) async-start(), calls=%async_computation.2 | async-start | bytes 1114112 | tf_op jit(solution)/shard_map/all_gather | solution.py:199
  22.2 124.1 %all-gather.7.cloned.1.call-start = ((), (), s32[]{:S(2)}) async-start(), calls=%async_computation.3 | async-start | bytes 1114112 | tf_op jit(solution)/shard_map/all_gather | solution.py:199
  63.7 2.1 copy-start
  69.3 2.1 copy-start
  98.9 11.5 %copy-start.3 = (f32[8,2048]{1,0:T(8,128)S(1)}, f32[8,2048]{1,0:T(8,128)}, u32[]{:S(2)}) copy-start(f32[8,2048]{1,0:T(8,128)} %param.15) | copy-start | bytes 196612
  146.3 2.1 copy-start.1
  152.0 2.1 copy-start.1
  159.0 41.4 %all-to-all-start.1 = ((f32[16,1,128]{2,1,0:T(1,128)}), f32[16,1,128]{2,1,0:T(1,128)S(1)}, u32[]{:S(2)}, u32[]{:S(2)}) async-start(f32[16,1,128]{2,1,0:T(1,128)} %reshape.2307), calls=%async_computation.1 | async-start | bytes 16384 | tf_op jit(solution)/shard_map/all_to_all | solution.py:218
  188.2 11.5 %copy-start.2 = (f32[8,2048]{1,0:T(8,128)S(1)}, f32[8,2048]{1,0:T(8,128)}, u32[]{:S(2)}) copy-start(f32[8,2048]{1,0:T(8,128)} %multiply_add_fusion.5) | copy-start | bytes 196612
Sparse Core Ops, SparseCore 0:
  24.4 39.2 all-gather.4
  111.2 35.0 all-gather.6
